TPU v7x, 32 devices: a whole 2x2x4 slice. The times are simulated.
32 devices in a mesh: groups: 2 (over x), ctx: 16 (over z, y, core).
Axes of the slice: x: 2, y: 2, z: 4, core: 2. Of those that a mesh axis runs over, the one named last changes fastest.
Arguments:
- signal_spectrum: bfloat16 [2, 8192, 4096], P(None, ('groups', 'ctx')), parts along dimension 1, may hold values from -6 to 6
- filter_spectrum: bfloat16 [2, 4096, 4096], P(None, 'ctx'), may hold values from -6 to 6
- output_gate: bfloat16 [4096, 4096], P(('groups', 'ctx')), parts along dimension 0, may hold values from -8 to 8
- projection: bfloat16 [4096, 384], replicated, may hold values from -0.5 to 0.5
Outputs:
- attended: bfloat16 [4096, 128], P(('groups', 'ctx')), parts along dimension 0
There are 2 independent parts, one for each index of `groups`. A program takes and returns all parts, laid end to end along the dimension named above; an argument that names none is the same for every part. Nothing has to cross between parts.
All inputs are finite; a program needn't handle non-finite values.
Results may differ from a plain program's by a relative error of at most 0.019.
Values may be sent and summed in bfloat16 or wider, within the bound.
No kernel may reach another device: no remote copies, remote signals or barrier semaphores. Data moves between devices by JAX's collectives and lax.ppermute only.
A program may use at most 128 MiB of HBM per device.

v0:
```python
import math
import jax
import jax.numpy as jnp
from jax import lax
from jax.sharding import PartitionSpec as P

TWO_PI = 2.0 * math.pi
FLOOR = -1e30
HIGHEST = lax.Precision.HIGHEST


def unit_circle(numerator, modulus):
    phases = TWO_PI / modulus * numerator.astype(jnp.float32)
    return (jnp.cos(phases), jnp.sin(phases))


def across_sources(pieces, span_total):
    sources = pieces.shape[2]
    freq_count = pieces.shape[3]
    form = "ud,cdp->cup"
    ordinal = jnp.arange(sources, dtype=jnp.int32)
    cos_table, sin_table = unit_circle(ordinal[:, None] * ordinal[None, :] % sources, sources)
    real_mid = jnp.einsum(form, cos_table, pieces[0], precision=HIGHEST) - jnp.einsum(
        form, sin_table, pieces[1], precision=HIGHEST
    )
    imag_mid = jnp.einsum(form, sin_table, pieces[0], precision=HIGHEST) + jnp.einsum(
        form, cos_table, pieces[1], precision=HIGHEST
    )
    freq_ids = jnp.arange(freq_count, dtype=jnp.int32)
    turn_cos, turn_sin = unit_circle(ordinal[:, None] * freq_ids[None, :] % span_total, span_total)
    turn_cos = turn_cos[None, :, :]
    turn_sin = turn_sin[None, :, :]
    real_out = real_mid * turn_cos - imag_mid * turn_sin
    imag_out = real_mid * turn_sin + imag_mid * turn_cos
    return jnp.stack([real_out, imag_out])


def across_freqs(pieces, out_rows, freq_count, span_total, form):
    row_ids = jnp.arange(out_rows, dtype=jnp.int32)
    freq_ids = jnp.arange(freq_count, dtype=jnp.int32)
    cos_table, sin_table = unit_circle(
        row_ids[:, None] * freq_ids[None, :] % freq_count, freq_count
    )
    result = jnp.einsum(form, cos_table, pieces[0], precision=HIGHEST) - jnp.einsum(
        form, sin_table, pieces[1], precision=HIGHEST
    )
    return result * (1.0 / math.sqrt(span_total))


def per_device(signal_spectrum, filter_spectrum, output_gate, projection):
    axis_count = lax.axis_size("ctx")
    me_index = lax.axis_index("ctx")
    rows_dev = output_gate.shape[0]
    freqs_dev = signal_spectrum.shape[1]
    span_total = axis_count * freqs_dev
    head_size = projection.shape[1] // 3
    local_rows = jnp.arange(rows_dev, dtype=jnp.int32)
    query_pos = me_index * rows_dev + local_rows
    signal = signal_spectrum.astype(jnp.float32)
    kernel = filter_spectrum.astype(jnp.float32)
    product = jnp.stack(
        [
            signal[0] * kernel[0] - signal[1] * kernel[1],
            signal[0] * kernel[1] + signal[1] * kernel[0],
        ]
    )
    chan_count = product.shape[2] // axis_count
    turned = jnp.swapaxes(product, 1, 2)
    gathered_freqs = lax.all_to_all(turned, "ctx", split_axis=1, concat_axis=2, tiled=True)
    pieces = gathered_freqs.reshape(2, chan_count, axis_count, freqs_dev)
    spread = across_sources(pieces, span_total)
    form = "vp,cup->vuc"
    mixed_rows = across_freqs(spread, rows_dev, freqs_dev, span_total, form)
    mixed_rows = lax.all_to_all(
        mixed_rows.reshape(axis_count, rows_dev, chan_count),
        "ctx",
        split_axis=0,
        concat_axis=2,
        tiled=True,
    ).reshape(rows_dev, -1)
    gated = (mixed_rows * output_gate.astype(jnp.float32)).astype(jnp.bfloat16)
    packed = jnp.dot(gated, projection, preferred_element_type=jnp.float32)
    query_rows = packed[:, :head_size].astype(jnp.bfloat16)
    key_rows = packed[:, head_size : 2 * head_size].astype(jnp.bfloat16)
    value_rows = packed[:, 2 * head_size :].astype(jnp.bfloat16)
    score_scale = 1.0 / math.sqrt(head_size)
    top_query = jnp.max(query_pos)

    def absorb_block(carried, key_part, value_part, first_key):
        key_index = first_key + jnp.arange(key_part.shape[0], dtype=jnp.int32)

        def update(current):
            running_max, totals, weighted = current
            scores = (
                jnp.einsum("qh,kh->qk", query_rows, key_part, preferred_element_type=jnp.float32)
                * score_scale
            )
            allowed = key_index[None, :] <= query_pos[:, None]
            scores = jnp.where(allowed, scores, FLOOR)
            new_max = jnp.maximum(running_max, jnp.max(scores, axis=1))
            exponents = jnp.where(allowed, jnp.exp(scores - new_max[:, None]), 0.0)
            factor = jnp.exp(running_max - new_max)
            totals = totals * factor + jnp.sum(exponents, axis=1)
            weighted = weighted * factor[:, None] + jnp.dot(
                exponents.astype(jnp.bfloat16), value_part, preferred_element_type=jnp.float32
            )
            return (new_max, totals, weighted)

        def unchanged(current):
            return current

        return lax.cond(jnp.min(key_index) > top_query, unchanged, update, carried)

    def absorb(carried, pieces, first_row):
        key_part, value_part = pieces
        key_total = key_part.shape[0]
        block_rows = 2048 if key_total > 2048 and key_total % 2048 == 0 else key_total
        if block_rows == key_total:
            return absorb_block(carried, key_part, value_part, first_row)
        block_count = key_total // block_rows
        key_blocks = key_part.reshape(block_count, block_rows, -1)
        value_blocks = value_part.reshape(block_count, block_rows, -1)
        offsets = first_row + block_rows * jnp.arange(block_count, dtype=jnp.int32)

        def step_block(current, inputs):
            return (absorb_block(current, inputs[0], inputs[1], inputs[2]), None)

        final_state, unused = lax.scan(step_block, carried, (key_blocks, value_blocks, offsets))
        return final_state

    initial = (
        jnp.full((rows_dev,), FLOOR, jnp.float32),
        jnp.zeros((rows_dev,), jnp.float32),
        jnp.zeros((rows_dev, head_size), jnp.float32),
    )
    running_max, totals, weighted = absorb(
        initial,
        (
            lax.all_gather(key_rows, "ctx", axis=0, tiled=True),
            lax.all_gather(value_rows, "ctx", axis=0, tiled=True),
        ),
        jnp.int32(0),
    )
    attended = (weighted / totals[:, None]).astype(jnp.bfloat16)
    return attended


def solution(mesh):
    in_specs = (
        P(None, ("groups", "ctx"), None),
        P(None, "ctx", None),
        P(("groups", "ctx"), None),
        P(),
    )
    out_specs = P(("groups", "ctx"), None)
    return jax.shard_map(
        per_device, mesh=mesh, in_specs=in_specs, out_specs=out_specs, check_vma=False
    )
```

profile of v0, /device:TPU:0, one launch (start us, length us, event | category | flops | bytes accessed | tf_op | source)
XLA Modules:
  0.0 387.8 jit_solution(934145070185385344)
XLA Ops:
  0.0 0.0 copy-start
  0.0 11.3 %copy.21 = bf16[2,256,4096]{1,0,2:T(2,128)(2,1)} copy(bf16[2,256,4096]{2,1,0:T(8,128)(2,1)} %param.6) | data formatting | bytes 8388608 | tf_op args[0]
  11.3 6.6 %convert_element_type.55 = f32[2,256,4096]{1,0,2:T(2,128)} convert(bf16[2,256,4096]{1,0,2:T(2,128)(2,1)} %copy.21) | non-fusion elementwise | flops 2097152 | bytes 12582912 | tf_op jit(solution)/shard_map/convert_element_type | solution.py:59
  17.9 11.1 %copy.22 = bf16[2,256,4096]{1,0,2:T(2,128)(2,1)} copy(bf16[2,256,4096]{2,1,0:T(8,128)(2,1)} %param.7) | data formatting | bytes 8388608 | tf_op args[1]
  29.1 0.0 copy-start.1
  29.1 5.2 %convert_element_type.56 = f32[2,256,4096]{1,0,2:T(2,128)S(1)} convert(bf16[2,256,4096]{1,0,2:T(2,128)(2,1)} %copy.22) | non-fusion elementwise | flops 2097152 | bytes 12582912 | tf_op jit(solution)/shard_map/convert_element_type | solution.py:60
  34.2 0.0 copy-done.1
  34.2 10.9 %multiply_subtract_fusion = (f32[1,256,4096]{1,0,2:T(1,128)S(1)}, f32[1,256,4096]{1,0,2:T(1,128)S(1)}) fusion(f32[2,256,4096]{1,0,2:T(2,128)S(1)} %convert_element_type.56, f32[2,256,4096]{1,0,2:T(2,128)S(1)} %copy-done.1), kind=kLoop, calls=%fused_computation.30 | loop fusion | flops 6291456 | bytes 25165824 | tf_op jit(solution)/shard_map/sub | solution.py:63
  45.2 8.7 %maximum_bitcast_fusion = f32[2,4096,256]{2,0,1:T(2,128)} fusion(f32[1,256,4096]{1,0,2:T(1,128)S(1)} %get-tuple-element.30, f32[1,256,4096]{1,0,2:T(1,128)S(1)} %get-tuple-element.29), kind=kLoop, calls=%fused_computation.15 | loop fusion | flops 2097152 | bytes 16777216 | tf_op jit(solution)/shard_map/transpose | solution.py:68
  53.9 8.0 %all-to-all-start = ((f32[2,4096,256]{2,0,1:T(2,128)}), f32[2,4096,256]{2,0,1:T(2,128)}, u32[]{:S(2)}, u32[]{:S(2)}) async-start(f32[2,4096,256]{2,0,1:T(2,128)} %maximum_bitcast_fusion), calls=%async_computation | async-start | bytes 16777216 | tf_op jit(solution)/shard_map/all_to_all | solution.py:69
  61.9 0.1 fusion.51
  62.0 150.0 %all-to-all-done = f32[2,4096,256]{2,0,1:T(2,128)} async-done(((f32[2,4096,256]{2,0,1:T(2,128)}), f32[2,4096,256]{2,0,1:T(2,128)}, u32[]{:S(2)}, u32[]{:S(2)}) %all-to-all-start) | async-done | bytes 8388640 | tf_op jit(solution)/shard_map/all_to_all | solution.py:69
  212.0 8.2 %copy.39 = f32[2,16,256,256]{3,1,2,0:T(8,128)S(1)} copy(f32[2,16,256,256]{3,0,2,1:T(2,128)} %bitcast.1) | data formatting | bytes 16777216 | tf_op jit(solution)/shard_map/all_to_all | solution.py:69
  220.2 4.1 %fusion.18 = f32[256,256,16]{1,2,0:T(8,128)S(1)} fusion(f32[2,256,16,256]{3,2,1,0:T(8,128)S(1)} %bitcast.66), kind=kOutput, calls=%fused_computation.32 | convolution fusion | flops 201330176 | bytes 8388608 | tf_op jit(solution)/shard_map/ud,cdp->cup/dot_general | solution.py:23
  224.3 4.3 %fusion.17 = f32[256,256,16]{1,2,0:T(8,128)S(1)} fusion(f32[2,256,16,256]{3,2,1,0:T(8,128)S(1)} %bitcast.67), kind=kOutput, calls=%fused_computation.31 | convolution fusion | flops 201330176 | bytes 8388608 | tf_op jit(solution)/shard_map/ud,cdp->cup/dot_general | solution.py:26
  228.6 4.1 %fusion.21 = f32[256,256,16]{1,2,0:T(8,128)S(1)} fusion(f32[256,256,16]{1,2,0:T(8,128)S(1)} %fusion.18, f32[2,256,16,256]{3,2,1,0:T(8,128)S(1)} %bitcast.68), kind=kOutput, calls=%fused_computation.35 | convolution fusion | flops 202378752 | bytes 12582912 | tf_op jit(solution)/shard_map/ud,cdp->cup/dot_general | solution.py:23
  232.7 5.1 %fusion.11 = (f32[256,16,256]{2,1,0:T(8,128)S(1)}, f32[256,16,256]{2,1,0:T(8,128)S(1)}) fusion(f32[256,256,16]{1,2,0:T(8,128)S(1)} %fusion.21, f32[16,256]{1,0:T(8,128)S(1)} %get-tuple-element.35, f32[16,256]{1,0:T(8,128)S(1)} %get-tuple-element.36, f32[256,256,16]{1,2,0:T(8,128)S(1)} %fusion.17, f32[2,256,16,256]{3,2,1,0:T(8,128)S(1)} %bitcast.69), kind=kOutput, calls=%fused_computation.21 | convolution fusion | flops 208670208 | bytes 21004288 | tf_op jit(solution)/shard_map/ud,cdp->cup/dot_general | solution.py:26
  237.8 7.4 %fusion.13 = f32[256,16,128]{0,2,1:T(8,128)S(1)} fusion(f32[256,16,256]{2,1,0:T(8,128)S(1)} %get-tuple-element.32), kind=kOutput, calls=%fused_computation.25 | convolution fusion | flops 1611071488 | bytes 6291456 | tf_op jit(solution)/shard_map/vp,cup->vuc/dot_general | solution.py:44
  245.3 7.3 %multiply_bitcast_fusion = f32[128,16,256]{2,0,1:T(8,128)S(1)} fusion(f32[256,16,128]{0,2,1:T(8,128)S(1)} %fusion.13, f32[256,16,256]{2,1,0:T(8,128)S(1)} %get-tuple-element.31), kind=kOutput, calls=%fused_computation.39 | convolution fusion | flops 1612120064 | bytes 8388608 | tf_op jit(solution)/shard_map/vp,cup->vuc/dot_general | solution.py:44
  252.5 2.5 copy.27
  255.0 36.5 %all-to-all-start.1 = ((f32[16,128,256]{2,1,0:T(8,128)}), f32[16,128,256]{2,1,0:T(8,128)}, u32[]{:S(2)}, u32[]{:S(2)}) async-start(f32[16,128,256]{2,1,0:T(8,128)} %bitcast.70), calls=%async_computation.1 | async-start | bytes 4194304 | tf_op jit(solution)/shard_map/all_to_all | solution.py:74
  291.6 2.3 copy.29
  293.9 0.6 fusion.86
  295.2 37.5 %all-to-all-done.1 = f32[16,128,256]{2,1,0:T(8,128)} async-done(((f32[16,128,256]{2,1,0:T(8,128)}), f32[16,128,256]{2,1,0:T(8,128)}, u32[]{:S(2)}, u32[]{:S(2)}) %all-to-all-start.1) | async-done | bytes 2097184 | tf_op jit(solution)/shard_map/all_to_all | solution.py:74
  332.6 2.9 copy.28
  335.5 2.1 fusion.23
  337.6 0.0 copy-done
  337.6 0.8 convolution_convert_fusion
  338.3 28.5 %all_gather.6 = bf16[2048,128]{1,0:T(8,128)(2,1)S(1)} all-gather(bf16[128,128]{1,0:T(8,128)(2,1)S(1)} %get-tuple-element.34), channel_id=1, replica_groups=mesh['groups'=2,'ctx'=16] {'ctx'}, dimensions={0}, use_global_device_ids=true | all-gather | bytes 557056 | tf_op jit(solution)/shard_map/all_gather | solution.py:139
  366.8 18.9 %all_gather.7 = bf16[2048,128]{1,0:T(8,128)(2,1)S(1)} all-gather(bf16[128,128]{1,0:T(8,128)(2,1)S(1)} %get-tuple-element.33), channel_id=1, replica_groups=mesh['groups'=2,'ctx'=16] {'ctx'}, dimensions={0}, use_global_device_ids=true | all-gather | bytes 557056 | tf_op jit(solution)/shard_map/all_gather | solution.py:140
  385.7 1.2 conditional.1
  385.7 0.4 fusion.87
  386.1 0.4 fusion.2
  386.4 0.4 convolution_add_fusion
  386.8 0.7 divide_convert_fusion
  (5 shorter events, 0.0 us)
Async XLA Ops:
  0.0 337.6 %copy-start = (bf16[4096,384]{1,0:T(8,128)(2,1)S(1)}, bf16[4096,384]{1,0:T(8,128)(2,1)}, u32[]{:S(2)}) copy-start(bf16[4096,384]{1,0:T(8,128)(2,1)} %param.9) | copy-start | bytes 9437188
  29.1 5.2 %copy-start.1 = (f32[2,256,4096]{1,0,2:T(2,128)S(1)}, f32[2,256,4096]{1,0,2:T(2,128)}, u32[]{:S(2)}) copy-start(f32[2,256,4096]{1,0,2:T(2,128)} %convert_element_type.55) | copy-start | bytes 25165828
  53.9 158.0 %all-to-all-start = ((f32[2,4096,256]{2,0,1:T(2,128)}), f32[2,4096,256]{2,0,1:T(2,128)}, u32[]{:S(2)}, u32[]{:S(2)}) async-start(f32[2,4096,256]{2,0,1:T(2,128)} %maximum_bitcast_fusion), calls=%async_computation | async-start | bytes 16777216 | tf_op jit(solution)/shard_map/all_to_all | solution.py:69
  255.0 77.6 %all-to-all-start.1 = ((f32[16,128,256]{2,1,0:T(8,128)}), f32[16,128,256]{2,1,0:T(8,128)}, u32[]{:S(2)}, u32[]{:S(2)}) async-start(f32[16,128,256]{2,1,0:T(8,128)} %bitcast.70), calls=%async_computation.1 | async-start | bytes 4194304 | tf_op jit(solution)/shard_map/all_to_all | solution.py:74
where the time goes:
time: 392 us; the launch traced here: 388 us
  waiting for transfers between devices  187 us (48%)
  blocking collectives  47.3 us (12%)
  starting transfers between devices  44.5 us (11%)
  local copies, waits for them, and re-layouts  38.4 us (10%)
  other arithmetic  35.3 us (9%)
  matrix products  33.8 us (9%)
    all_to_all x1, waiting for transfers between devices, per_device(): lax.all_to_all(turned, 'ctx', split_axis=1, concat_axis=2, tiled=True)  150 us
    all_to_all x1, waiting for transfers between devices, per_device(): lax.all_to_all(mixed_rows.reshape(axis_count, rows_dev, chan_count), 'ctx...  37.5 us
    all_to_all x1, starting transfers between devices, per_device(): lax.all_to_all(mixed_rows.reshape(axis_count, rows_dev, chan_count), 'ctx...  36.5 us
    all_gather x1, blocking collectives, per_device(): lax.all_gather(key_rows, 'ctx', axis=0, tiled=True)  28.5 us
    unnamed x7, local copies, waits for them, and re-layouts  24.7 us
    all_gather x1, blocking collectives, per_device(): lax.all_gather(value_rows, 'ctx', axis=0, tiled=True)  18.9 us
    sub x1, other arithmetic, per_device(): signal[0] * kernel[0] - signal[1] * kernel[1]  10.9 us
    transpose x1, other arithmetic, per_device(): turned = jnp.swapaxes(product, 1, 2)  8.75 us
  transfers between devices with their start and end apart: 2, of which 2 were waited for; matrix products, arithmetic and copies ran while one was open for 1% of the time, Pallas kernels for 0%

commit v1 on v0

--- a/solution.py
+++ b/solution.py
@@ -7,6 +7,25 @@
 TWO_PI = 2.0 * math.pi
 FLOOR = -1e30
 HIGHEST = lax.Precision.HIGHEST
+
+
+def balance_space(panel, group_axis, array_axis):
+    all_values = jax.lax.psum(1, axis_name=group_axis)
+    vec_out = jax.lax.axis_index(group_axis)
+    new, long_array, m_next = (all_values, vec_out, panel.shape[array_axis])
+    trail = [dd * new if u == array_axis else dd for u, dd in enumerate(panel.shape)]
+    piece_out = jnp.zeros(trail, panel.dtype)
+    block_now = lax.dynamic_update_slice_in_dim(
+        piece_out, panel, long_array * m_next, axis=array_axis
+    )
+    for i in range(1, new):
+        panel = jax.lax.ppermute(
+            panel, axis_name=group_axis, perm=[(u, (u + 1) % new) for u in range(new)]
+        )
+        block_now = lax.dynamic_update_slice_in_dim(
+            block_now, panel, (long_array - i) % new * m_next, axis=array_axis
+        )
+    return block_now
 
 
 def unit_circle(numerator, modulus):
@@ -135,10 +154,7 @@
     )
     running_max, totals, weighted = absorb(
         initial,
-        (
-            lax.all_gather(key_rows, "ctx", axis=0, tiled=True),
-            lax.all_gather(value_rows, "ctx", axis=0, tiled=True),
-        ),
+        (balance_space(key_rows, "ctx", 0), lax.all_gather(value_rows, "ctx", axis=0, tiled=True)),
         jnp.int32(0),
     )
     attended = (weighted / totals[:, None]).astype(jnp.bfloat16)

time: 392 us -> 480 us (1.22)
  waiting for transfers between devices: 187 us -> 277 us
  blocking collectives: 47.3 us -> 20.8 us
  local copies, waits for them, and re-layouts: 38.4 us -> 58.4 us
    ppermute x0 -> x15, waiting for transfers between devices: none -> 88.2 us  [balance_space(): jax.lax.ppermute(panel, axis_name=group_axis, perm=[(u, (u + 1) % new) fo...]
    all_gather x1 -> x0, blocking collectives: 28.5 us -> none  [per_device(): lax.all_gather(key_rows, 'ctx', axis=0, tiled=True)]
    dynamic_update_slice x0 -> x16, local copies, waits for them, and re-layouts: none -> 16.7 us  [the longest x15 15.2 us: balance_space(): lax.dynamic_update_slice_in_dim(block_now, panel, (long_array - i) % new...]
    unnamed x7 -> x15, local copies, waits for them, and re-layouts: 24.7 us -> 27.2 us
  transfers between devices with their start and end apart: 2 -> 17, of which waited for: 2 -> 16; matrix products, arithmetic and copies ran while one was open for 1% -> 1% of each run, Pallas kernels for 0% -> 0%
where the time goes in v1:
time: 480 us; the launch traced here: 475 us
  waiting for transfers between devices  277 us (58%)
  local copies, waits for them, and re-layouts  58.4 us (12%)
  starting transfers between devices  45.6 us (10%)
  matrix products  36.3 us (8%)
  other arithmetic  35.5 us (7%)
  blocking collectives  20.8 us (4%)
    all_to_all x1, waiting for transfers between devices, per_device(): lax.all_to_all(turned, 'ctx', split_axis=1, concat_axis=2, tiled=True)  150 us
    ppermute x15, waiting for transfers between devices, balance_space(): jax.lax.ppermute(panel, axis_name=group_axis, perm=[(u, (u + 1) % new) fo...  88.2 us
    all_to_all x1, waiting for transfers between devices, per_device(): lax.all_to_all(mixed_rows.reshape(axis_count, rows_dev, chan_count), 'ctx...  38.7 us
    all_to_all x1, starting transfers between devices, per_device(): lax.all_to_all(mixed_rows.reshape(axis_count, rows_dev, chan_count), 'ctx...  36.5 us
    unnamed x15, local copies, waits for them, and re-layouts  27.2 us
    all_gather x1, blocking collectives, per_device(): lax.all_gather(value_rows, 'ctx', axis=0, tiled=True)  20.8 us
    dynamic_update_slice x15, local copies, waits for them, and re-layouts, balance_space(): lax.dynamic_update_slice_in_dim(block_now, panel, (long_array - i) % new...  15.2 us
    sub x1, other arithmetic, per_device(): signal[0] * kernel[0] - signal[1] * kernel[1]  10.9 us
  transfers between devices with their start and end apart: 17, of which 16 were waited for; matrix products, arithmetic and copies ran while one was open for 1% of the time, Pallas kernels for 0%

profile of v1, /device:TPU:0, one launch (start us, length us, event | category | flops | bytes accessed | tf_op | source)
XLA Modules:
  0.0 474.7 jit_solution(5989156318004918940)
XLA Ops:
  0.0 11.3 %copy.21 = bf16[2,256,4096]{1,0,2:T(2,128)(2,1)} copy(bf16[2,256,4096]{2,1,0:T(8,128)(2,1)} %param.6) | data formatting | bytes 8388608 | tf_op args[0]
  11.3 6.7 %convert_element_type.58 = f32[2,256,4096]{1,0,2:T(2,128)} convert(bf16[2,256,4096]{1,0,2:T(2,128)(2,1)} %copy.21) | non-fusion elementwise | flops 2097152 | bytes 12582912 | tf_op jit(solution)/shard_map/convert_element_type | solution.py:78
  18.0 11.1 %copy.22 = bf16[2,256,4096]{1,0,2:T(2,128)(2,1)} copy(bf16[2,256,4096]{2,1,0:T(8,128)(2,1)} %param.7) | data formatting | bytes 8388608 | tf_op args[1]
  29.1 5.2 %convert_element_type.59 = f32[2,256,4096]{1,0,2:T(2,128)S(1)} convert(bf16[2,256,4096]{1,0,2:T(2,128)(2,1)} %copy.22) | non-fusion elementwise | flops 2097152 | bytes 12582912 | tf_op jit(solution)/shard_map/convert_element_type | solution.py:79
  34.3 10.9 %multiply_subtract_fusion = (f32[1,256,4096]{1,0,2:T(1,128)S(1)}, f32[1,256,4096]{1,0,2:T(1,128)S(1)}) fusion(f32[2,256,4096]{1,0,2:T(2,128)S(1)} %convert_element_type.59, f32[2,256,4096]{1,0,2:T(2,128)S(1)} %copy-done.1), kind=kLoop, calls=%fused_computation.46 | loop fusion | flops 6291456 | bytes 25165824 | tf_op jit(solution)/shard_map/sub | solution.py:82
  45.2 8.7 %maximum_bitcast_fusion = f32[2,4096,256]{2,0,1:T(2,128)} fusion(f32[1,256,4096]{1,0,2:T(1,128)S(1)} %get-tuple-element.1496, f32[1,256,4096]{1,0,2:T(1,128)S(1)} %get-tuple-element.1495), kind=kLoop, calls=%fused_computation.31 | loop fusion | flops 2097152 | bytes 16777216 | tf_op jit(solution)/shard_map/transpose | solution.py:87
  53.9 8.0 %all-to-all-start = ((f32[2,4096,256]{2,0,1:T(2,128)}), f32[2,4096,256]{2,0,1:T(2,128)}, u32[]{:S(2)}, u32[]{:S(2)}) async-start(f32[2,4096,256]{2,0,1:T(2,128)} %maximum_bitcast_fusion), calls=%async_computation | async-start | bytes 16777216 | tf_op jit(solution)/shard_map/all_to_all | solution.py:88
  62.0 150.0 %all-to-all-done = f32[2,4096,256]{2,0,1:T(2,128)} async-done(((f32[2,4096,256]{2,0,1:T(2,128)}), f32[2,4096,256]{2,0,1:T(2,128)}, u32[]{:S(2)}, u32[]{:S(2)}) %all-to-all-start) | async-done | bytes 8388640 | tf_op jit(solution)/shard_map/all_to_all | solution.py:88
  212.0 8.2 %copy.39 = f32[2,16,256,256]{3,1,2,0:T(8,128)S(1)} copy(f32[2,16,256,256]{3,0,2,1:T(2,128)} %bitcast.1) | data formatting | bytes 16777216 | tf_op jit(solution)/shard_map/all_to_all | solution.py:88
  220.2 4.1 fusion.19
  224.3 4.3 fusion.18
  228.6 4.1 fusion.22
  232.7 5.1 %fusion.12 = (f32[256,16,256]{2,1,0:T(8,128)S(1)}, f32[256,16,256]{2,1,0:T(8,128)S(1)}) fusion(f32[256,256,16]{1,2,0:T(8,128)S(1)} %fusion.22, f32[16,256]{1,0:T(8,128)S(1)} %get-tuple-element.1501, f32[16,256]{1,0:T(8,128)S(1)} %get-tuple-element.1502, f32[256,256,16]{1,2,0:T(8,128)S(1)} %fusion.18, f32[2,256,16,256]{3,2,1,0:T(8,128)S(1)} %bitcast.74), kind=kOutput, calls=%fused_computation.37 | convolution fusion | flops 208670208 | bytes 21004288 | tf_op jit(solution)/shard_map/ud,cdp->cup/dot_general | solution.py:45
  237.8 7.4 %fusion.14 = f32[256,16,128]{0,2,1:T(8,128)S(1)} fusion(f32[256,16,256]{2,1,0:T(8,128)S(1)} %get-tuple-element.1498), kind=kOutput, calls=%fused_computation.41 | convolution fusion | flops 1611071488 | bytes 6291456 | tf_op jit(solution)/shard_map/vp,cup->vuc/dot_general | solution.py:63
  245.3 7.3 %multiply_bitcast_fusion = f32[128,16,256]{2,0,1:T(8,128)S(1)} fusion(f32[256,16,128]{0,2,1:T(8,128)S(1)} %fusion.14, f32[256,16,256]{2,1,0:T(8,128)S(1)} %get-tuple-element.1497), kind=kOutput, calls=%fused_computation.55 | convolution fusion | flops 1612120064 | bytes 8388608 | tf_op jit(solution)/shard_map/vp,cup->vuc/dot_general | solution.py:63
  252.5 2.5 copy.27
  255.1 36.5 %all-to-all-start.1 = ((f32[16,128,256]{2,1,0:T(8,128)}), f32[16,128,256]{2,1,0:T(8,128)}, u32[]{:S(2)}, u32[]{:S(2)}) async-start(f32[16,128,256]{2,1,0:T(8,128)} %bitcast.75), calls=%async_computation.1 | async-start | bytes 4194304 | tf_op jit(solution)/shard_map/all_to_all | solution.py:93
  291.6 2.3 copy.29
  293.9 38.7 %all-to-all-done.1 = f32[16,128,256]{2,1,0:T(8,128)} async-done(((f32[16,128,256]{2,1,0:T(8,128)}), f32[16,128,256]{2,1,0:T(8,128)}, u32[]{:S(2)}, u32[]{:S(2)}) %all-to-all-start.1) | async-done | bytes 2097184 | tf_op jit(solution)/shard_map/all_to_all | solution.py:93
  332.6 2.9 copy.28
  335.5 2.1 fusion.24
  337.6 0.8 convolution_convert_fusion
  338.4 1.0 collective-permute-start
  339.4 10.5 %collective-permute-done = bf16[128,128]{1,0:T(8,128)(2,1)S(1)} collective-permute-done((bf16[128,128]{1,0:T(8,128)(2,1)S(1)}, bf16[128,128]{1,0:T(8,128)(2,1)S(1)}, u32[]{:S(2)}, u32[]{:S(2)}) %collective-permute-start) | collective-permute-done | bytes 32800 | tf_op jit(solution)/shard_map/ppermute | solution.py:22
  349.9 6.0 %collective-permute-done.1 = bf16[128,128]{1,0:T(8,128)(2,1)S(1)} collective-permute-done((bf16[128,128]{1,0:T(8,128)(2,1)S(1)}, bf16[128,128]{1,0:T(8,128)(2,1)S(1)}, u32[]{:S(2)}, u32[]{:S(2)}) %collective-permute-start.1) | collective-permute-done | bytes 32800 | tf_op jit(solution)/shard_map/ppermute | solution.py:22
  355.9 6.0 %collective-permute-done.2 = bf16[128,128]{1,0:T(8,128)(2,1)S(1)} collective-permute-done((bf16[128,128]{1,0:T(8,128)(2,1)S(1)}, bf16[128,128]{1,0:T(8,128)(2,1)S(1)}, u32[]{:S(2)}, u32[]{:S(2)}) %collective-permute-start.2) | collective-permute-done | bytes 32800 | tf_op jit(solution)/shard_map/ppermute | solution.py:22
  361.9 6.0 %collective-permute-done.3 = bf16[128,128]{1,0:T(8,128)(2,1)S(1)} collective-permute-done((bf16[128,128]{1,0:T(8,128)(2,1)S(1)}, bf16[128,128]{1,0:T(8,128)(2,1)S(1)}, u32[]{:S(2)}, u32[]{:S(2)}) %collective-permute-start.3) | collective-permute-done | bytes 32800 | tf_op jit(solution)/shard_map/ppermute | solution.py:22
  368.0 6.0 %collective-permute-done.4 = bf16[128,128]{1,0:T(8,128)(2,1)S(1)} collective-permute-done((bf16[128,128]{1,0:T(8,128)(2,1)S(1)}, bf16[128,128]{1,0:T(8,128)(2,1)S(1)}, u32[]{:S(2)}, u32[]{:S(2)}) %collective-permute-start.4) | collective-permute-done | bytes 32800 | tf_op jit(solution)/shard_map/ppermute | solution.py:22
  374.0 6.0 %collective-permute-done.5 = bf16[128,128]{1,0:T(8,128)(2,1)S(1)} collective-permute-done((bf16[128,128]{1,0:T(8,128)(2,1)S(1)}, bf16[128,128]{1,0:T(8,128)(2,1)S(1)}, u32[]{:S(2)}, u32[]{:S(2)}) %collective-permute-start.5) | collective-permute-done | bytes 32800 | tf_op jit(solution)/shard_map/ppermute | solution.py:22
  380.1 6.0 %collective-permute-done.6 = bf16[128,128]{1,0:T(8,128)(2,1)S(1)} collective-permute-done((bf16[128,128]{1,0:T(8,128)(2,1)S(1)}, bf16[128,128]{1,0:T(8,128)(2,1)S(1)}, u32[]{:S(2)}, u32[]{:S(2)}) %collective-permute-start.6) | collective-permute-done | bytes 32800 | tf_op jit(solution)/shard_map/ppermute | solution.py:22
  386.1 6.0 %collective-permute-done.7 = bf16[128,128]{1,0:T(8,128)(2,1)S(1)} collective-permute-done((bf16[128,128]{1,0:T(8,128)(2,1)S(1)}, bf16[128,128]{1,0:T(8,128)(2,1)S(1)}, u32[]{:S(2)}, u32[]{:S(2)}) %collective-permute-start.7) | collective-permute-done | bytes 32800 | tf_op jit(solution)/shard_map/ppermute | solution.py:22
  392.1 0.6 copy-done.2
  392.7 6.0 %collective-permute-done.8 = bf16[128,128]{1,0:T(8,128)(2,1)S(1)} collective-permute-done((bf16[128,128]{1,0:T(8,128)(2,1)S(1)}, bf16[128,128]{1,0:T(8,128)(2,1)S(1)}, u32[]{:S(2)}, u32[]{:S(2)}) %collective-permute-start.8) | collective-permute-done | bytes 32800 | tf_op jit(solution)/shard_map/ppermute | solution.py:22
  398.8 0.6 copy-done.3
  399.4 6.0 %collective-permute-done.9 = bf16[128,128]{1,0:T(8,128)(2,1)S(1)} collective-permute-done((bf16[128,128]{1,0:T(8,128)(2,1)S(1)}, bf16[128,128]{1,0:T(8,128)(2,1)S(1)}, u32[]{:S(2)}, u32[]{:S(2)}) %collective-permute-start.9) | collective-permute-done | bytes 32800 | tf_op jit(solution)/shard_map/ppermute | solution.py:22
  405.4 0.6 copy-done.4
  406.0 6.0 %collective-permute-done.10 = bf16[128,128]{1,0:T(8,128)(2,1)S(1)} collective-permute-done((bf16[128,128]{1,0:T(8,128)(2,1)S(1)}, bf16[128,128]{1,0:T(8,128)(2,1)S(1)}, u32[]{:S(2)}, u32[]{:S(2)}) %collective-permute-start.10) | collective-permute-done | bytes 32800 | tf_op jit(solution)/shard_map/ppermute | solution.py:22
  412.1 0.6 copy-done.5
  412.7 6.1 %collective-permute-done.11 = bf16[128,128]{1,0:T(8,128)(2,1)} collective-permute-done((bf16[128,128]{1,0:T(8,128)(2,1)S(1)}, bf16[128,128]{1,0:T(8,128)(2,1)}, u32[]{:S(2)}, u32[]{:S(2)}) %collective-permute-start.11) | collective-permute-done | bytes 32800 | tf_op jit(solution)/shard_map/ppermute | solution.py:22
  418.8 6.3 %collective-permute-done.12 = bf16[128,128]{1,0:T(8,128)(2,1)} collective-permute-done((bf16[128,128]{1,0:T(8,128)(2,1)}, bf16[128,128]{1,0:T(8,128)(2,1)}, u32[]{:S(2)}, u32[]{:S(2)}) %collective-permute-start.12) | collective-permute-done | bytes 32800 | tf_op jit(solution)/shard_map/ppermute | solution.py:22
  425.2 0.7 fusion.87
  426.6 4.9 %collective-permute-done.13 = bf16[128,128]{1,0:T(8,128)(2,1)} collective-permute-done((bf16[128,128]{1,0:T(8,128)(2,1)}, bf16[128,128]{1,0:T(8,128)(2,1)}, u32[]{:S(2)}, u32[]{:S(2)}) %collective-permute-start.13) | collective-permute-done | bytes 32800 | tf_op jit(solution)/shard_map/ppermute | solution.py:22
  431.5 20.8 %all_gather.3 = bf16[2048,128]{1,0:T(8,128)(2,1)} all-gather(bf16[128,128]{1,0:T(8,128)(2,1)S(1)} %get-tuple-element.1499), channel_id=1, replica_groups=mesh['groups'=2,'ctx'=16] {'ctx'}, dimensions={0}, use_global_device_ids=true | all-gather | bytes 557056 | tf_op jit(solution)/shard_map/all_gather | solution.py:157
  452.4 21.3 %conditional.1 = (f32[128]{0:T(128)S(1)}, f32[128,128]{1,0:T(8,128)S(1)}) conditional(s32[]{:T(128)} %convert_element_type.57, (s32[2048]{0:T(1024)S(1)}, s32[128]{0:T(128)S(1)}, s32[]{:T(128)}, bf16[128,128]{1,0:T(8,128)(2,1)S(1)}, s32[]{:T(128)}, /*index=5*/bf16[128,128]{1,0:T(8,128)(2,1)S(1)}, s32[]{:T(128)}, ...), branch_computations={%region_1.4_spmd.clone.clone, %region_4.5_spmd} | conditional | flops 137380464 | bytes 5899837 | solution.py:131
  452.4 0.9 broadcast_in_dim.58
  453.2 1.4 dynamic_update_slice.160
  454.7 0.6 constant_dynamic-update-slice_fusion.14
  455.3 0.6 constant_dynamic-update-slice_fusion.13
  455.9 0.6 constant_dynamic-update-slice_fusion.12
  456.5 0.6 constant_dynamic-update-slice_fusion.11
  457.1 0.6 constant_dynamic-update-slice_fusion.10
  457.7 0.6 constant_dynamic-update-slice_fusion.9
  458.3 0.6 constant_dynamic-update-slice_fusion.8
  459.0 1.4 constant_dynamic-update-slice_fusion.7
  460.3 1.4 constant_dynamic-update-slice_fusion.6
  461.7 1.4 constant_dynamic-update-slice_fusion.5
  463.1 1.4 constant_dynamic-update-slice_fusion.4
  464.5 1.4 constant_dynamic-update-slice_fusion.3
  465.8 1.4 constant_dynamic-update-slice_fusion.2
  467.2 1.4 constant_dynamic-update-slice_fusion.1
  468.6 1.4 constant_dynamic-update-slice_fusion
  469.9 1.6 fusion.88
  472.0 1.7 convolution_add_fusion
  473.7 0.7 divide_convert_fusion
  (30 shorter events, 0.6 us)
Async XLA Ops:
  0.0 337.6 %copy-start = (bf16[4096,384]{1,0:T(8,128)(2,1)S(1)}, bf16[4096,384]{1,0:T(8,128)(2,1)}, u32[]{:S(2)}) copy-start(bf16[4096,384]{1,0:T(8,128)(2,1)} %param.9) | copy-start | bytes 9437188
  29.1 5.2 %copy-start.1 = (f32[2,256,4096]{1,0,2:T(2,128)S(1)}, f32[2,256,4096]{1,0,2:T(2,128)}, u32[]{:S(2)}) copy-start(f32[2,256,4096]{1,0,2:T(2,128)} %convert_element_type.58) | copy-start | bytes 25165828
  53.9 158.0 %all-to-all-start = ((f32[2,4096,256]{2,0,1:T(2,128)}), f32[2,4096,256]{2,0,1:T(2,128)}, u32[]{:S(2)}, u32[]{:S(2)}) async-start(f32[2,4096,256]{2,0,1:T(2,128)} %maximum_bitcast_fusion), calls=%async_computation | async-start | bytes 16777216 | tf_op jit(solution)/shard_map/all_to_all | solution.py:88
  255.1 77.6 %all-to-all-start.1 = ((f32[16,128,256]{2,1,0:T(8,128)}), f32[16,128,256]{2,1,0:T(8,128)}, u32[]{:S(2)}, u32[]{:S(2)}) async-start(f32[16,128,256]{2,1,0:T(8,128)} %bitcast.75), calls=%async_computation.1 | async-start | bytes 4194304 | tf_op jit(solution)/shard_map/all_to_all | solution.py:93
  338.4 11.5 %collective-permute-start = (bf16[128,128]{1,0:T(8,128)(2,1)S(1)}, bf16[128,128]{1,0:T(8,128)(2,1)S(1)}, u32[]{:S(2)}, u32[]{:S(2)}) collective-permute-start(bf16[128,128]{1,0:T(8,128)(2,1)S(1)} %get-tuple-element.1500), channel_id=1, source_target_pairs={{0,1},{1,2},{2,3},{3,4},{4,5},{5,6},{6,7},{7,8},{8,9},{9,10},{10,1... | collective-permute-start | bytes 98312 | tf_op jit(solution)/shard_map/ppermute | solution.py:22
  349.9 6.0 %collective-permute-start.1 = (bf16[128,128]{1,0:T(8,128)(2,1)S(1)}, bf16[128,128]{1,0:T(8,128)(2,1)S(1)}, u32[]{:S(2)}, u32[]{:S(2)}) collective-permute-start(bf16[128,128]{1,0:T(8,128)(2,1)S(1)} %collective-permute-done), channel_id=1, source_target_pairs={{0,1},{1,2},{2,3},{3,4},{4,5},{5,6},{6,7},{7,8},{8,9},{9,10},{10,1... | collective-permute-start | bytes 98312 | tf_op jit(solution)/shard_map/ppermute | solution.py:22
  355.9 6.0 %collective-permute-start.2 = (bf16[128,128]{1,0:T(8,128)(2,1)S(1)}, bf16[128,128]{1,0:T(8,128)(2,1)S(1)}, u32[]{:S(2)}, u32[]{:S(2)}) collective-permute-start(bf16[128,128]{1,0:T(8,128)(2,1)S(1)} %collective-permute-done.1), channel_id=1, source_target_pairs={{0,1},{1,2},{2,3},{3,4},{4,5},{5,6},{6,7},{7,8},{8,9},{9,10},{10,1... | collective-permute-start | bytes 98312 | tf_op jit(solution)/shard_map/ppermute | solution.py:22
  361.9 6.0 %collective-permute-start.3 = (bf16[128,128]{1,0:T(8,128)(2,1)S(1)}, bf16[128,128]{1,0:T(8,128)(2,1)S(1)}, u32[]{:S(2)}, u32[]{:S(2)}) collective-permute-start(bf16[128,128]{1,0:T(8,128)(2,1)S(1)} %collective-permute-done.2), channel_id=1, source_target_pairs={{0,1},{1,2},{2,3},{3,4},{4,5},{5,6},{6,7},{7,8},{8,9},{9,10},{10,1... | collective-permute-start | bytes 98312 | tf_op jit(solution)/shard_map/ppermute | solution.py:22
  368.0 6.0 %collective-permute-start.4 = (bf16[128,128]{1,0:T(8,128)(2,1)S(1)}, bf16[128,128]{1,0:T(8,128)(2,1)S(1)}, u32[]{:S(2)}, u32[]{:S(2)}) collective-permute-start(bf16[128,128]{1,0:T(8,128)(2,1)S(1)} %collective-permute-done.3), channel_id=1, source_target_pairs={{0,1},{1,2},{2,3},{3,4},{4,5},{5,6},{6,7},{7,8},{8,9},{9,10},{10,1... | collective-permute-start | bytes 98312 | tf_op jit(solution)/shard_map/ppermute | solution.py:22
  374.0 6.0 %collective-permute-start.5 = (bf16[128,128]{1,0:T(8,128)(2,1)S(1)}, bf16[128,128]{1,0:T(8,128)(2,1)S(1)}, u32[]{:S(2)}, u32[]{:S(2)}) collective-permute-start(bf16[128,128]{1,0:T(8,128)(2,1)S(1)} %collective-permute-done.4), channel_id=1, source_target_pairs={{0,1},{1,2},{2,3},{3,4},{4,5},{5,6},{6,7},{7,8},{8,9},{9,10},{10,1... | collective-permute-start | bytes 98312 | tf_op jit(solution)/shard_map/ppermute | solution.py:22
  380.0 6.0 %collective-permute-start.6 = (bf16[128,128]{1,0:T(8,128)(2,1)S(1)}, bf16[128,128]{1,0:T(8,128)(2,1)S(1)}, u32[]{:S(2)}, u32[]{:S(2)}) collective-permute-start(bf16[128,128]{1,0:T(8,128)(2,1)S(1)} %collective-permute-done.5), channel_id=1, source_target_pairs={{0,1},{1,2},{2,3},{3,4},{4,5},{5,6},{6,7},{7,8},{8,9},{9,10},{10,1... | collective-permute-start | bytes 98312 | tf_op jit(solution)/shard_map/ppermute | solution.py:22
  386.1 6.0 %collective-permute-start.7 = (bf16[128,128]{1,0:T(8,128)(2,1)S(1)}, bf16[128,128]{1,0:T(8,128)(2,1)S(1)}, u32[]{:S(2)}, u32[]{:S(2)}) collective-permute-start(bf16[128,128]{1,0:T(8,128)(2,1)S(1)} %collective-permute-done.6), channel_id=1, source_target_pairs={{0,1},{1,2},{2,3},{3,4},{4,5},{5,6},{6,7},{7,8},{8,9},{9,10},{10,1... | collective-permute-start | bytes 98312 | tf_op jit(solution)/shard_map/ppermute | solution.py:22
  392.1 0.6 copy-start.2
  392.7 6.0 %collective-permute-start.8 = (bf16[128,128]{1,0:T(8,128)(2,1)S(1)}, bf16[128,128]{1,0:T(8,128)(2,1)S(1)}, u32[]{:S(2)}, u32[]{:S(2)}) collective-permute-start(bf16[128,128]{1,0:T(8,128)(2,1)S(1)} %collective-permute-done.7), channel_id=1, source_target_pairs={{0,1},{1,2},{2,3},{3,4},{4,5},{5,6},{6,7},{7,8},{8,9},{9,10},{10,1... | collective-permute-start | bytes 98312 | tf_op jit(solution)/shard_map/ppermute | solution.py:22
  398.8 0.6 copy-start.3
  399.4 6.0 %collective-permute-start.9 = (bf16[128,128]{1,0:T(8,128)(2,1)S(1)}, bf16[128,128]{1,0:T(8,128)(2,1)S(1)}, u32[]{:S(2)}, u32[]{:S(2)}) collective-permute-start(bf16[128,128]{1,0:T(8,128)(2,1)S(1)} %collective-permute-done.8), channel_id=1, source_target_pairs={{0,1},{1,2},{2,3},{3,4},{4,5},{5,6},{6,7},{7,8},{8,9},{9,10},{10,1... | collective-permute-start | bytes 98312 | tf_op jit(solution)/shard_map/ppermute | solution.py:22
  405.4 0.6 copy-start.4
  406.0 6.0 %collective-permute-start.10 = (bf16[128,128]{1,0:T(8,128)(2,1)S(1)}, bf16[128,128]{1,0:T(8,128)(2,1)S(1)}, u32[]{:S(2)}, u32[]{:S(2)}) collective-permute-start(bf16[128,128]{1,0:T(8,128)(2,1)S(1)} %collective-permute-done.9), channel_id=1, source_target_pairs={{0,1},{1,2},{2,3},{3,4},{4,5},{5,6},{6,7},{7,8},{8,9},{9,10},{10,1... | collective-permute-start | bytes 98312 | tf_op jit(solution)/shard_map/ppermute | solution.py:22
  412.1 0.6 copy-start.5
  412.7 6.1 %collective-permute-start.11 = (bf16[128,128]{1,0:T(8,128)(2,1)S(1)}, bf16[128,128]{1,0:T(8,128)(2,1)}, u32[]{:S(2)}, u32[]{:S(2)}) collective-permute-start(bf16[128,128]{1,0:T(8,128)(2,1)S(1)} %collective-permute-done.10), channel_id=1, source_target_pairs={{0,1},{1,2},{2,3},{3,4},{4,5},{5,6},{6,7},{7,8},{8,9},{9,10},{10,1... | collective-permute-start | bytes 98312 | tf_op jit(solution)/shard_map/ppermute | solution.py:22
  418.8 6.4 %collective-permute-start.12 = (bf16[128,128]{1,0:T(8,128)(2,1)}, bf16[128,128]{1,0:T(8,128)(2,1)}, u32[]{:S(2)}, u32[]{:S(2)}) collective-permute-start(bf16[128,128]{1,0:T(8,128)(2,1)} %collective-permute-done.11), channel_id=1, source_target_pairs={{0,1},{1,2},{2,3},{3,4},{4,5},{5,6},{6,7},{7,8},{8,9},{9,10},{10,1... | collective-permute-start | bytes 98312 | tf_op jit(solution)/shard_map/ppermute | solution.py:22
  425.2 6.4 %collective-permute-start.13 = (bf16[128,128]{1,0:T(8,128)(2,1)}, bf16[128,128]{1,0:T(8,128)(2,1)}, u32[]{:S(2)}, u32[]{:S(2)}) collective-permute-start(bf16[128,128]{1,0:T(8,128)(2,1)} %collective-permute-done.12), channel_id=1, source_target_pairs={{0,1},{1,2},{2,3},{3,4},{4,5},{5,6},{6,7},{7,8},{8,9},{9,10},{10,1... | collective-permute-start | bytes 98312 | tf_op jit(solution)/shard_map/ppermute | solution.py:22
  431.5 20.8 %collective-permute-start.14 = (bf16[128,128]{1,0:T(8,128)(2,1)}, bf16[128,128]{1,0:T(8,128)(2,1)}, u32[]{:S(2)}, u32[]{:S(2)}) collective-permute-start(bf16[128,128]{1,0:T(8,128)(2,1)} %collective-permute-done.13), channel_id=1, source_target_pairs={{0,1},{1,2},{2,3},{3,4},{4,5},{5,6},{6,7},{7,8},{8,9},{9,10},{10,1... | collective-permute-start | bytes 98312 | tf_op jit(solution)/shard_map/ppermute | solution.py:22
